TPU v7x, 32 devices: a whole 2x2x4 slice. The times are simulated.
32 devices in a mesh: path: 4 (over z), trade: 8 (over y, x, core).
Axes of the slice: x: 2, y: 2, z: 4, core: 2. Of those that a mesh axis runs over, the one named last changes fastest.
Arguments:
- factors: bfloat16 [32, 8, 512], P(None, None, 'path'), may hold values from -5 to 5
- loadings: bfloat16 [32, 8, 32768], P(None, None, 'trade'), may hold values from -0.5 to 0.5
- notional: float32 [32768], P('trade'), may hold values from -1 to 1
- strike: float32 [32768], P('trade'), may hold values from 0.5 to 1.5
- date_weight: float32 [32], replicated, may hold values from 0.3 to 3
- loss_spanning: float32 [128], replicated, may hold values from 0.2 to 0.9
- loss_local: float32 [1024], P('trade'), may hold values from 0.2 to 0.9
- trade_slot: int32 [32768], P('trade'), may hold values from 0 to 255
- span_list: int32 [1024], P('trade'), may hold values from 0 to 127, as said below
Outputs:
- loading_grad: float32 [32, 8, 32768], P('path', None, 'trade')
- factor_grad: float32 [32, 8, 512], P('trade', None, 'path')
Inputs may be any that keep to these rules, and one draw needn't show every extreme that they name: `trade_slot`: slot s < 128 of a trade shard holds that shard's spanning set from span_list; slot 128 + i holds the shard's i-th local set. `span_list`: the 128 entries of one trade shard are distinct spanning set ids.
All inputs are finite; a program needn't handle non-finite values.
Results may differ from a plain program's by a relative error of at most 0.0021.
Values may be sent and summed in bfloat16 or wider, within the bound.
A program may use at most 64 MiB of HBM per device.

v0:
```python
import math
import jax
import jax.numpy as jnp
from jax import lax
from jax.sharding import PartitionSpec as P

smoothing = 0.5


def price(factor_block, loading_block):
    exponent = jnp.einsum(
        "bfp,bfk->bpk", factor_block, loading_block, preferred_element_type=jnp.float32
    )
    return jnp.exp(exponent)


def on_device(
    factors,
    loadings,
    notional,
    strike,
    date_weight,
    loss_spanning,
    loss_local,
    trade_slot,
    span_list,
):
    path_total = lax.axis_size("path") * factors.shape[2]
    factor_here = lax.all_to_all(factors, "path", split_axis=0, concat_axis=2, tiled=True)
    dates_here = factor_here.shape[0]
    first_date = lax.axis_index("path") * dates_here
    loading_here = lax.dynamic_slice_in_dim(loadings, first_date, dates_here, 0)
    weight_here = lax.dynamic_slice_in_dim(date_weight, first_date, dates_here, 0)
    date_count = factor_here.shape[0]
    factor_count = factor_here.shape[1]
    path_local = factor_here.shape[2]
    trade_local = loading_here.shape[2]
    span_local = span_list.shape[0]
    span_count = loss_spanning.shape[0]
    slot_count = span_local + loss_local.shape[0]
    dates_per_step = math.gcd(date_count, max(1, 512 // path_local))
    block_count = date_count // dates_per_step
    slot_table = (trade_slot[:, None] == jnp.arange(slot_count, dtype=jnp.int32)[None, :]).astype(
        jnp.bfloat16
    )
    set_match = span_list[:, None] == jnp.arange(span_count, dtype=jnp.int32)[None, :]
    set_table = set_match.astype(jnp.float32)
    set_select = set_match.astype(jnp.bfloat16)
    factor_blocks = factor_here.reshape(block_count, dates_per_step, factor_count, path_local)
    loading_blocks = loading_here.reshape(block_count, dates_per_step, factor_count, trade_local)
    weight_blocks = weight_here.reshape(block_count, dates_per_step)

    def forward(operands):
        factor_block, loading_block, weight_block = operands
        growth = price(factor_block, loading_block)
        values = (notional * (growth - strike)).astype(jnp.bfloat16)
        partial_sums = jnp.einsum(
            "bpk,ks->bps", values, slot_table, preferred_element_type=jnp.float32
        )
        span_part = jnp.einsum(
            "bps,sn->bpn",
            partial_sums[:, :, :span_local],
            set_table,
            precision=lax.Precision.HIGHEST,
            preferred_element_type=jnp.float32,
        )
        local_weight = (
            weight_block[:, None, None]
            * loss_local
            * jax.nn.sigmoid(partial_sums[:, :, span_local:] / smoothing)
        ).astype(jnp.bfloat16)
        return (span_part, local_weight)

    span_parts, local_weights = lax.map(forward, (factor_blocks, loading_blocks, weight_blocks))
    span_parts = span_parts.reshape(date_count, path_local, span_count)
    span_total = lax.psum(span_parts, "trade")
    span_weight = (
        weight_here[:, None, None] * loss_spanning * jax.nn.sigmoid(span_total / smoothing)
    ).astype(jnp.bfloat16)
    span_blocks = span_weight.reshape(block_count, dates_per_step, path_local, span_count)

    def adjoint(operands):
        factor_block, loading_block, span_block, local_block = operands
        growth = price(factor_block, loading_block)
        span_slots = jnp.einsum(
            "bpn,sn->bps", span_block, set_select, preferred_element_type=jnp.float32
        ).astype(jnp.bfloat16)
        slot_weight = jnp.concatenate([span_slots, local_block], axis=2)
        trade_weight = jnp.einsum(
            "bps,ks->bpk", slot_weight, slot_table, preferred_element_type=jnp.float32
        )
        sensitivity = (trade_weight * notional * growth).astype(jnp.bfloat16)
        loading_term = jnp.einsum(
            "bfp,bpk->bfk", factor_block, sensitivity, preferred_element_type=jnp.float32
        )
        factor_term = jnp.einsum(
            "bfk,bpk->bfp", loading_block, sensitivity, preferred_element_type=jnp.float32
        )
        return (loading_term, factor_term)

    loading_terms, factor_terms = lax.map(
        adjoint, (factor_blocks, loading_blocks, span_blocks, local_weights)
    )
    loading_terms = loading_terms.reshape(date_count, factor_count, trade_local)
    factor_terms = factor_terms.reshape(date_count, factor_count, path_local)
    loading_grad = loading_terms / path_total
    regrouped = lax.all_to_all(factor_terms, "path", split_axis=2, concat_axis=0, tiled=True)
    factor_grad = lax.psum_scatter(regrouped, "trade", scatter_dimension=0, tiled=True)
    return (loading_grad, factor_grad)


def solution(mesh):
    return jax.shard_map(
        on_device,
        mesh=mesh,
        in_specs=(
            P(None, None, "path"),
            P(None, None, "trade"),
            P("trade"),
            P("trade"),
            P(),
            P(),
            P("trade"),
            P("trade"),
            P("trade"),
        ),
        out_specs=(P("path", None, "trade"), P("trade", None, "path")),
        check_vma=False,
    )
```

profile of v0, /device:TPU:0, one launch (start us, length us, event | category | flops | bytes accessed | tf_op | source)
XLA Modules:
  0.0 284.7 jit_solution(14998099556894631179)
XLA Ops:
  7.2 6.5 %all-to-all-start = ((bf16[32,8,128]{2,1,0:T(8,128)(2,1)}), bf16[32,8,128]{2,1,0:T(8,128)(2,1)S(1)}, u32[]{:S(2)}, u32[]{:S(2)}) async-start(bf16[32,8,128]{2,1,0:T(8,128)(2,1)} %param.13), calls=%async_computation | async-start | bytes 131072 | tf_op jit(solution)/shard_map/all_to_all | solution.py:29
  14.5 4.9 %all-to-all-done = bf16[32,8,128]{2,1,0:T(8,128)(2,1)S(1)} async-done(((bf16[32,8,128]{2,1,0:T(8,128)(2,1)}), bf16[32,8,128]{2,1,0:T(8,128)(2,1)S(1)}, u32[]{:S(2)}, u32[]{:S(2)}) %all-to-all-start) | async-done | bytes 65568 | tf_op jit(solution)/shard_map/all_to_all | solution.py:29
  19.5 50.6 %while.26 = (s32[]{:T(128)}, f32[8,1,512,128]{3,2,1,0:T(8,128)}, bf16[8,1,512,128]{3,2,1,0:T(8,128)(2,1)}, f32[4096]{0:T(1024)}, bf16[8,1,8,512]{3,2,1,0:T(8,128...) while((s32[]{:T(128)}, f32[8,1,512,128]{3,2,1,0:T(8,128)}, ...), condition=%wide.region_1.2_spmd.clone, body=%wide.region_0.1_spmd.clone.sunk | while | flops 1216774272 | bytes 1573053 | solution.py:74
  19.5 3.3 %fusion.88 = f32[1,512,256]{2,1,0:T(8,128)S(1)} fusion(s32[4096]{0:T(1024)} %get-tuple-element.392, f32[4096]{0:T(1024)} %get-tuple-element.389, f32[4096]{0:T(1024)} %get-tuple-element.386, bf16[8,1,8,4096]{3,2,1,0:T(8,128)(2,1)S(1)} %get-tuple-element.388, s32[]{:T(128)} %get-tuple-element.371, bf16[8,1,8,512]{3,2,1,0:T(8,128)(2,1)S(1)} %get-tuple-element.387), kind=kOutput, calls=%fused_computation.9.clone.1 | convolution fusion | flops 1115684864 | bytes 648192 | tf_op jit(solution)/shard_map/while/body/eval_jaxpr/bpk,ks->bps/dot_general | solution.py:57
  25.8 3.3 %fusion.88 = f32[1,512,256]{2,1,0:T(8,128)S(1)} fusion(s32[4096]{0:T(1024)} %get-tuple-element.392, f32[4096]{0:T(1024)} %get-tuple-element.389, f32[4096]{0:T(1024)} %get-tuple-element.386, bf16[8,1,8,4096]{3,2,1,0:T(8,128)(2,1)S(1)} %get-tuple-element.388, s32[]{:T(128)} %get-tuple-element.371, bf16[8,1,8,512]{3,2,1,0:T(8,128)(2,1)S(1)} %get-tuple-element.387), kind=kOutput, calls=%fused_computation.9.clone.1 | convolution fusion | flops 1115684864 | bytes 648192 | tf_op jit(solution)/shard_map/while/body/eval_jaxpr/bpk,ks->bps/dot_general | solution.py:57
  32.1 3.3 %fusion.88 = f32[1,512,256]{2,1,0:T(8,128)S(1)} fusion(s32[4096]{0:T(1024)} %get-tuple-element.392, f32[4096]{0:T(1024)} %get-tuple-element.389, f32[4096]{0:T(1024)} %get-tuple-element.386, bf16[8,1,8,4096]{3,2,1,0:T(8,128)(2,1)S(1)} %get-tuple-element.388, s32[]{:T(128)} %get-tuple-element.371, bf16[8,1,8,512]{3,2,1,0:T(8,128)(2,1)S(1)} %get-tuple-element.387), kind=kOutput, calls=%fused_computation.9.clone.1 | convolution fusion | flops 1115684864 | bytes 648192 | tf_op jit(solution)/shard_map/while/body/eval_jaxpr/bpk,ks->bps/dot_general | solution.py:57
  38.4 3.3 %fusion.88 = f32[1,512,256]{2,1,0:T(8,128)S(1)} fusion(s32[4096]{0:T(1024)} %get-tuple-element.392, f32[4096]{0:T(1024)} %get-tuple-element.389, f32[4096]{0:T(1024)} %get-tuple-element.386, bf16[8,1,8,4096]{3,2,1,0:T(8,128)(2,1)S(1)} %get-tuple-element.388, s32[]{:T(128)} %get-tuple-element.371, bf16[8,1,8,512]{3,2,1,0:T(8,128)(2,1)S(1)} %get-tuple-element.387), kind=kOutput, calls=%fused_computation.9.clone.1 | convolution fusion | flops 1115684864 | bytes 648192 | tf_op jit(solution)/shard_map/while/body/eval_jaxpr/bpk,ks->bps/dot_general | solution.py:57
  44.7 3.3 %fusion.88 = f32[1,512,256]{2,1,0:T(8,128)S(1)} fusion(s32[4096]{0:T(1024)} %get-tuple-element.392, f32[4096]{0:T(1024)} %get-tuple-element.389, f32[4096]{0:T(1024)} %get-tuple-element.386, bf16[8,1,8,4096]{3,2,1,0:T(8,128)(2,1)S(1)} %get-tuple-element.388, s32[]{:T(128)} %get-tuple-element.371, bf16[8,1,8,512]{3,2,1,0:T(8,128)(2,1)S(1)} %get-tuple-element.387), kind=kOutput, calls=%fused_computation.9.clone.1 | convolution fusion | flops 1115684864 | bytes 648192 | tf_op jit(solution)/shard_map/while/body/eval_jaxpr/bpk,ks->bps/dot_general | solution.py:57
  51.0 3.3 %fusion.88 = f32[1,512,256]{2,1,0:T(8,128)S(1)} fusion(s32[4096]{0:T(1024)} %get-tuple-element.392, f32[4096]{0:T(1024)} %get-tuple-element.389, f32[4096]{0:T(1024)} %get-tuple-element.386, bf16[8,1,8,4096]{3,2,1,0:T(8,128)(2,1)S(1)} %get-tuple-element.388, s32[]{:T(128)} %get-tuple-element.371, bf16[8,1,8,512]{3,2,1,0:T(8,128)(2,1)S(1)} %get-tuple-element.387), kind=kOutput, calls=%fused_computation.9.clone.1 | convolution fusion | flops 1115684864 | bytes 648192 | tf_op jit(solution)/shard_map/while/body/eval_jaxpr/bpk,ks->bps/dot_general | solution.py:57
  57.3 3.3 %fusion.88 = f32[1,512,256]{2,1,0:T(8,128)S(1)} fusion(s32[4096]{0:T(1024)} %get-tuple-element.392, f32[4096]{0:T(1024)} %get-tuple-element.389, f32[4096]{0:T(1024)} %get-tuple-element.386, bf16[8,1,8,4096]{3,2,1,0:T(8,128)(2,1)S(1)} %get-tuple-element.388, s32[]{:T(128)} %get-tuple-element.371, bf16[8,1,8,512]{3,2,1,0:T(8,128)(2,1)S(1)} %get-tuple-element.387), kind=kOutput, calls=%fused_computation.9.clone.1 | convolution fusion | flops 1115684864 | bytes 648192 | tf_op jit(solution)/shard_map/while/body/eval_jaxpr/bpk,ks->bps/dot_general | solution.py:57
  63.7 3.3 %fusion.88 = f32[1,512,256]{2,1,0:T(8,128)S(1)} fusion(s32[4096]{0:T(1024)} %get-tuple-element.392, f32[4096]{0:T(1024)} %get-tuple-element.389, f32[4096]{0:T(1024)} %get-tuple-element.386, bf16[8,1,8,4096]{3,2,1,0:T(8,128)(2,1)S(1)} %get-tuple-element.388, s32[]{:T(128)} %get-tuple-element.371, bf16[8,1,8,512]{3,2,1,0:T(8,128)(2,1)S(1)} %get-tuple-element.387), kind=kOutput, calls=%fused_computation.9.clone.1 | convolution fusion | flops 1115684864 | bytes 648192 | tf_op jit(solution)/shard_map/while/body/eval_jaxpr/bpk,ks->bps/dot_general | solution.py:57
  70.9 59.7 %all-reduce.2.cloned.1.call-done = f32[8,512,128]{2,1,0:T(8,128)} async-done(((f32[8,512,128]{2,1,0:T(8,128)}), f32[8,512,128]{2,1,0:T(8,128)}) %all-reduce.2.cloned.1.call-update) | async-done | bytes 2097168 | tf_op jit(solution)/shard_map/psum | solution.py:76
  132.7 88.6 %while.27 = (s32[]{:T(128)}, f32[8,1,8,4096]{3,2,1,0:T(8,128)}, f32[8,1,8,512]{3,2,1,0:T(8,128)}, bf16[8,1,8,512]{3,2,1,0:T(8,128)(2,1)S(1)}, bf16[8,1,512,128]{...) while((s32[]{:T(128)}, f32[8,1,8,4096]{3,2,1,0:T(8,128)}, ...), condition=%wide.region_4.5_spmd.clone, body=%wide.region_3.4_spmd.clone.sunk | while | flops 1200193536 | bytes 31266512 | solution.py:101
  134.6 2.6 fusion.100
  141.1 2.6 fusion.102
  145.7 2.6 fusion.100
  156.7 2.6 fusion.100
  167.8 2.6 fusion.100
  174.3 2.6 fusion.102
  178.9 2.6 fusion.100
  189.9 2.6 fusion.100
  196.5 2.6 fusion.102
  201.0 2.6 fusion.100
  207.5 2.6 fusion.102
  212.1 2.6 fusion.100
  218.6 2.6 fusion.102
  221.3 2.9 %copy.18 = f32[8,1,8,512]{2,0,3,1:T(8,128)} copy(f32[8,1,8,512]{3,2,1,0:T(8,128)} %get-tuple-element.445) | data formatting | bytes 262144 | tf_op jit(solution)/shard_map/while | solution.py:101
  224.1 3.1 %bitcast_bitcast_fusion = f32[512,8,8]{2,1,0:T(8,128)} fusion(f32[8,1,8,512]{2,0,3,1:T(8,128)} %copy.18), kind=kLoop, calls=%fused_computation.71 | loop fusion | bytes 262144
  227.2 2.7 reshape.144
  229.8 10.2 %all_to_all.33 = f32[4,1,8192]{2,1,0:T(1,128)S(1)} all-to-all(f32[4,1,8192]{2,1,0:T(1,128)S(1)} %reshape.144), channel_id=1, replica_groups=mesh['path'=4,'trade'=8] {'path'}, dimensions={0} | all-to-all | bytes 262144 | tf_op jit(solution)/shard_map/all_to_all | solution.py:107
  244.1 2.8 copy.19
  249.2 28.7 %reduce-scatter.2.cloned.1.call-done = f32[4,8,128]{2,1,0:T(8,128)} async-done(((f32[32,8,128]{2,1,0:T(8,128)}), f32[4,8,128]{2,1,0:T(8,128)}) %reduce-scatter.2.cloned.1.call-update) | async-done | bytes 16400 | tf_op jit(solution)/shard_map/reduce_scatter | solution.py:108
  (185 shorter events, 88.0 us)
Async XLA Ops:
  7.2 6.5 %copy-start = (bf16[32,8,4096]{2,1,0:T(8,128)(2,1)S(1)}, bf16[32,8,4096]{2,1,0:T(8,128)(2,1)}, u32[]{:S(2)}) copy-start(bf16[32,8,4096]{2,1,0:T(8,128)(2,1)} %param.14) | copy-start | bytes 6291460
  7.2 12.2 %all-to-all-start = ((bf16[32,8,128]{2,1,0:T(8,128)(2,1)}), bf16[32,8,128]{2,1,0:T(8,128)(2,1)S(1)}, u32[]{:S(2)}, u32[]{:S(2)}) async-start(bf16[32,8,128]{2,1,0:T(8,128)(2,1)} %param.13), calls=%async_computation | async-start | bytes 131072 | tf_op jit(solution)/shard_map/all_to_all | solution.py:29
  13.7 116.8 %all-reduce.2.cloned.1.call-start = ((), (), s32[]{:S(2)}) async-start(), calls=%async_computation.3 | async-start | bytes 4194304 | tf_op jit(solution)/shard_map/psum | solution.py:76
  19.4 50.7 %copy-start.10 = (f32[32]{0:T(128)S(1)}, f32[32]{0:T(128)}, u32[]{:S(2)}) copy-start(f32[32]{0:T(128)} %param.17) | copy-start | bytes 388
  19.4 50.7 %copy-start.8 = (f32[128]{0:T(128)S(1)}, f32[128]{0:T(128)}, u32[]{:S(2)}) copy-start(f32[128]{0:T(128)} %param.18) | copy-start | bytes 1540
  19.5 3.9 %copy-start.9 = (f32[128]{0:T(128)S(1)}, f32[128]{0:T(128)}, u32[]{:S(2)}) copy-start(f32[128]{0:T(128)} %get-tuple-element.391) | copy-start | bytes 1540 | tf_op jit(solution)/shard_map/while
  19.5 5.2 %copy-start.5 = (s32[128]{0:T(128)S(1)}, s32[128]{0:T(128)}, u32[]{:S(2)}) copy-start(s32[128]{0:T(128)} %get-tuple-element.393) | copy-start | bytes 1540 | tf_op jit(solution)/shard_map/while
  25.8 3.9 %copy-start.9 = (f32[128]{0:T(128)S(1)}, f32[128]{0:T(128)}, u32[]{:S(2)}) copy-start(f32[128]{0:T(128)} %get-tuple-element.391) | copy-start | bytes 1540 | tf_op jit(solution)/shard_map/while
  25.8 5.2 %copy-start.5 = (s32[128]{0:T(128)S(1)}, s32[128]{0:T(128)}, u32[]{:S(2)}) copy-start(s32[128]{0:T(128)} %get-tuple-element.393) | copy-start | bytes 1540 | tf_op jit(solution)/shard_map/while
  32.1 3.9 %copy-start.9 = (f32[128]{0:T(128)S(1)}, f32[128]{0:T(128)}, u32[]{:S(2)}) copy-start(f32[128]{0:T(128)} %get-tuple-element.391) | copy-start | bytes 1540 | tf_op jit(solution)/shard_map/while
  32.1 5.2 %copy-start.5 = (s32[128]{0:T(128)S(1)}, s32[128]{0:T(128)}, u32[]{:S(2)}) copy-start(s32[128]{0:T(128)} %get-tuple-element.393) | copy-start | bytes 1540 | tf_op jit(solution)/shard_map/while
  38.4 3.9 %copy-start.9 = (f32[128]{0:T(128)S(1)}, f32[128]{0:T(128)}, u32[]{:S(2)}) copy-start(f32[128]{0:T(128)} %get-tuple-element.391) | copy-start | bytes 1540 | tf_op jit(solution)/shard_map/while
  38.4 5.1 %copy-start.5 = (s32[128]{0:T(128)S(1)}, s32[128]{0:T(128)}, u32[]{:S(2)}) copy-start(s32[128]{0:T(128)} %get-tuple-element.393) | copy-start | bytes 1540 | tf_op jit(solution)/shard_map/while
  44.7 3.9 %copy-start.9 = (f32[128]{0:T(128)S(1)}, f32[128]{0:T(128)}, u32[]{:S(2)}) copy-start(f32[128]{0:T(128)} %get-tuple-element.391) | copy-start | bytes 1540 | tf_op jit(solution)/shard_map/while
  44.7 5.2 %copy-start.5 = (s32[128]{0:T(128)S(1)}, s32[128]{0:T(128)}, u32[]{:S(2)}) copy-start(s32[128]{0:T(128)} %get-tuple-element.393) | copy-start | bytes 1540 | tf_op jit(solution)/shard_map/while
  51.0 3.9 %copy-start.9 = (f32[128]{0:T(128)S(1)}, f32[128]{0:T(128)}, u32[]{:S(2)}) copy-start(f32[128]{0:T(128)} %get-tuple-element.391) | copy-start | bytes 1540 | tf_op jit(solution)/shard_map/while
  51.0 5.2 %copy-start.5 = (s32[128]{0:T(128)S(1)}, s32[128]{0:T(128)}, u32[]{:S(2)}) copy-start(s32[128]{0:T(128)} %get-tuple-element.393) | copy-start | bytes 1540 | tf_op jit(solution)/shard_map/while
  57.3 3.9 %copy-start.9 = (f32[128]{0:T(128)S(1)}, f32[128]{0:T(128)}, u32[]{:S(2)}) copy-start(f32[128]{0:T(128)} %get-tuple-element.391) | copy-start | bytes 1540 | tf_op jit(solution)/shard_map/while
  57.3 5.2 %copy-start.5 = (s32[128]{0:T(128)S(1)}, s32[128]{0:T(128)}, u32[]{:S(2)}) copy-start(s32[128]{0:T(128)} %get-tuple-element.393) | copy-start | bytes 1540 | tf_op jit(solution)/shard_map/while
  63.7 3.9 %copy-start.9 = (f32[128]{0:T(128)S(1)}, f32[128]{0:T(128)}, u32[]{:S(2)}) copy-start(f32[128]{0:T(128)} %get-tuple-element.391) | copy-start | bytes 1540 | tf_op jit(solution)/shard_map/while
  63.7 5.2 %copy-start.5 = (s32[128]{0:T(128)S(1)}, s32[128]{0:T(128)}, u32[]{:S(2)}) copy-start(s32[128]{0:T(128)} %get-tuple-element.393) | copy-start | bytes 1540 | tf_op jit(solution)/shard_map/while
  70.0 62.6 %copy-start.2 = (f32[4096]{0:T(1024)S(1)}, f32[4096]{0:T(1024)}, u32[]{:S(2)}) copy-start(f32[4096]{0:T(1024)} %get-tuple-element.436) | copy-start | bytes 49156
  70.0 62.7 %copy-start.6 = (s32[128]{0:T(128)S(1)}, s32[128]{0:T(128)}, u32[]{:S(2)}) copy-start(s32[128]{0:T(128)} %get-tuple-element.442) | copy-start | bytes 1540
  70.0 207.8 %reduce-scatter.2.cloned.1.call-start = ((), (), s32[]{:S(2)}) async-start(), calls=%async_computation.4 | async-start | bytes 147456 | tf_op jit(solution)/shard_map/reduce_scatter | solution.py:108
  139.8 4.0 %copy-start.7 = (s32[128]{0:T(128)S(1)}, s32[128]{0:T(128)}, u32[]{:S(2)}) copy-start(s32[128]{0:T(128)} %get-tuple-element.454) | copy-start | bytes 1540 | tf_op jit(solution)/shard_map/while
  150.9 4.0 %copy-start.7 = (s32[128]{0:T(128)S(1)}, s32[128]{0:T(128)}, u32[]{:S(2)}) copy-start(s32[128]{0:T(128)} %get-tuple-element.454) | copy-start | bytes 1540 | tf_op jit(solution)/shard_map/while
  161.9 4.0 %copy-start.7 = (s32[128]{0:T(128)S(1)}, s32[128]{0:T(128)}, u32[]{:S(2)}) copy-start(s32[128]{0:T(128)} %get-tuple-element.454) | copy-start | bytes 1540 | tf_op jit(solution)/shard_map/while
  173.0 4.0 %copy-start.7 = (s32[128]{0:T(128)S(1)}, s32[128]{0:T(128)}, u32[]{:S(2)}) copy-start(s32[128]{0:T(128)} %get-tuple-element.454) | copy-start | bytes 1540 | tf_op jit(solution)/shard_map/while
  184.1 4.0 %copy-start.7 = (s32[128]{0:T(128)S(1)}, s32[128]{0:T(128)}, u32[]{:S(2)}) copy-start(s32[128]{0:T(128)} %get-tuple-element.454) | copy-start | bytes 1540 | tf_op jit(solution)/shard_map/while
  195.1 4.0 %copy-start.7 = (s32[128]{0:T(128)S(1)}, s32[128]{0:T(128)}, u32[]{:S(2)}) copy-start(s32[128]{0:T(128)} %get-tuple-element.454) | copy-start | bytes 1540 | tf_op jit(solution)/shard_map/while
  206.2 4.0 %copy-start.7 = (s32[128]{0:T(128)S(1)}, s32[128]{0:T(128)}, u32[]{:S(2)}) copy-start(s32[128]{0:T(128)} %get-tuple-element.454) | copy-start | bytes 1540 | tf_op jit(solution)/shard_map/while
  217.3 4.0 %copy-start.7 = (s32[128]{0:T(128)S(1)}, s32[128]{0:T(128)}, u32[]{:S(2)}) copy-start(s32[128]{0:T(128)} %get-tuple-element.454) | copy-start | bytes 1540 | tf_op jit(solution)/shard_map/while
  (17 other events, 26.3 us)
Sparse Core Ops, SparseCore 0:
  70.2 60.2 all-reduce.1
  247.0 30.8 reduce-scatter.1
where the time goes:
time: 287 us; the launch traced here: 285 us
  matrix products  110 us (38%)
  waiting for transfers between devices  93.3 us (33%)
  local copies, waits for them, and re-layouts  33.8 us (12%)
  other arithmetic  15.8 us (6%)
  between operations  14.1 us (5%)
  blocking collectives  10.2 us (4%)
  starting transfers between devices  6.53 us (2%)
    psum x1, waiting for transfers between devices, on_device(): span_total = lax.psum(span_parts, 'trade')  59.7 us
    reduce_scatter x1, waiting for transfers between devices, on_device(): lax.psum_scatter(regrouped, 'trade', scatter_dimension=0, tiled=True)  28.7 us
    dot_general x8, matrix products, forward(): jnp.einsum('bpk,ks->bps', values, slot_table, preferred_element_type=jnp....  26.4 us
    dot_general x8, matrix products, adjoint(): jnp.einsum('bps,ks->bpk', slot_weight, slot_table, preferred_element_type...  21.1 us
    dot_general x8, matrix products, adjoint(): jnp.einsum('bfk,bpk->bfp', loading_block, sensitivity, preferred_element_...  21.1 us
    dot_general x8, matrix products, price(): jnp.einsum('bfp,bfk->bpk', factor_block, loading_block, preferred_element...  20.3 us
    dot_general x8, matrix products, adjoint(): jnp.einsum('bfp,bpk->bfk', factor_block, sensitivity, preferred_element_t...  10.5 us
    all_to_all x1, blocking collectives, on_device(): lax.all_to_all(factor_terms, 'path', split_axis=2, concat_axis=0, tiled=T...  10.2 us
  transfers between devices with their start and end apart: 3, of which 3 were waited for; matrix products, arithmetic and copies ran while one was open for 1% of the time, Pallas kernels for 0%

commit v1 on v0

--- a/solution.py
+++ b/solution.py
@@ -73,7 +73,7 @@
 
     span_parts, local_weights = lax.map(forward, (factor_blocks, loading_blocks, weight_blocks))
     span_parts = span_parts.reshape(date_count, path_local, span_count)
-    span_total = lax.psum(span_parts, "trade")
+    span_total = jnp.sum(lax.all_gather(span_parts, "trade"), axis=0)
     span_weight = (
         weight_here[:, None, None] * loss_spanning * jax.nn.sigmoid(span_total / smoothing)
     ).astype(jnp.bfloat16)

time: 287 us -> 327 us (1.14)
  waiting for transfers between devices: 93.3 us -> 123 us
  other arithmetic: 15.8 us -> 24.6 us
  matrix products: 110 us -> 116 us
  local copies, waits for them, and re-layouts: 33.8 us -> 28.9 us
    all_gather x0 -> x1, waiting for transfers between devices: none -> 88 us  [on_device(): span_total = jnp.sum(lax.all_gather(span_parts, 'trade'), axis=0)]
    psum x1 -> x0, waiting for transfers between devices: 59.7 us -> none  [on_device(): span_total = lax.psum(span_parts, 'trade')]
    reduce_sum x0 -> x1, other arithmetic: none -> 8.28 us  [on_device(): span_total = jnp.sum(lax.all_gather(span_parts, 'trade'), axis=0)]
    dot_general x8, matrix products: 10.5 us -> 16.1 us  [adjoint(): jnp.einsum('bfp,bpk->bfk', factor_block, sensitivity, preferred_element_t...]
    while x80 -> x48, local copies, waits for them, and re-layouts: 5.19 us -> 0.11 us
    unnamed x15 -> x17, local copies, waits for them, and re-layouts: 8.86 us -> 8.26 us
where the time goes in v1:
time: 327 us; the launch traced here: 324 us
  waiting for transfers between devices  123 us (38%)
  matrix products  116 us (35%)
  local copies, waits for them, and re-layouts  28.9 us (9%)
  other arithmetic  24.6 us (8%)
  between operations  14.1 us (4%)
  blocking collectives  10.7 us (3%)
  starting transfers between devices  6.71 us (2%)
    all_gather x1, waiting for transfers between devices, on_device(): span_total = jnp.sum(lax.all_gather(span_parts, 'trade'), axis=0)  88 us
    reduce_scatter x1, waiting for transfers between devices, on_device(): lax.psum_scatter(regrouped, 'trade', scatter_dimension=0, tiled=True)  29.7 us
    dot_general x8, matrix products, forward(): jnp.einsum('bpk,ks->bps', values, slot_table, preferred_element_type=jnp....  26.4 us
    dot_general x8, matrix products, adjoint(): jnp.einsum('bps,ks->bpk', slot_weight, slot_table, preferred_element_type...  21.1 us
    dot_general x8, matrix products, adjoint(): jnp.einsum('bfk,bpk->bfp', loading_block, sensitivity, preferred_element_...  21 us
    dot_general x8, matrix products, price(): jnp.einsum('bfp,bfk->bpk', factor_block, loading_block, preferred_element...  20 us
    dot_general x8, matrix products, adjoint(): jnp.einsum('bfp,bpk->bfk', factor_block, sensitivity, preferred_element_t...  16.1 us
    all_to_all x1, blocking collectives, on_device(): lax.all_to_all(factor_terms, 'path', split_axis=2, concat_axis=0, tiled=T...  10.7 us
  transfers between devices with their start and end apart: 3, of which 3 were waited for; matrix products, arithmetic and copies ran while one was open for 1% of the time, Pallas kernels for 0%

profile of v1, /device:TPU:0, one launch (start us, length us, event | category | flops | bytes accessed | tf_op | source)
XLA Modules:
  0.0 323.8 jit_solution(11580717634521124922)
XLA Ops:
  7.2 6.5 %all-to-all-start = ((bf16[32,8,128]{2,1,0:T(8,128)(2,1)}), bf16[32,8,128]{2,1,0:T(8,128)(2,1)S(1)}, u32[]{:S(2)}, u32[]{:S(2)}) async-start(bf16[32,8,128]{2,1,0:T(8,128)(2,1)} %param.13), calls=%async_computation | async-start | bytes 131072 | tf_op jit(solution)/shard_map/all_to_all | solution.py:29
  14.5 4.9 %all-to-all-done = bf16[32,8,128]{2,1,0:T(8,128)(2,1)S(1)} async-done(((bf16[32,8,128]{2,1,0:T(8,128)(2,1)}), bf16[32,8,128]{2,1,0:T(8,128)(2,1)S(1)}, u32[]{:S(2)}, u32[]{:S(2)}) %all-to-all-start) | async-done | bytes 65568 | tf_op jit(solution)/shard_map/all_to_all | solution.py:29
  19.5 51.7 %while.26 = (s32[]{:T(128)}, f32[8,1,512,128]{3,2,1,0:T(8,128)}, bf16[8,1,512,128]{3,2,1,0:T(8,128)(2,1)}, f32[4096]{0:T(1024)}, bf16[8,1,8,512]{3,2,1,0:T(8,128...) while((s32[]{:T(128)}, f32[8,1,512,128]{3,2,1,0:T(8,128)}, ...), condition=%wide.region_1.2_spmd.clone, body=%wide.region_0.1_spmd.clone.sunk | while | flops 1216774272 | bytes 1573053 | solution.py:74
  19.5 3.3 %fusion.88 = f32[1,512,256]{2,1,0:T(8,128)S(1)} fusion(s32[4096]{0:T(1024)} %get-tuple-element.392, f32[4096]{0:T(1024)} %get-tuple-element.389, f32[4096]{0:T(1024)} %get-tuple-element.386, bf16[8,1,8,4096]{3,2,1,0:T(8,128)(2,1)S(1)} %get-tuple-element.388, s32[]{:T(128)} %get-tuple-element.371, bf16[8,1,8,512]{3,2,1,0:T(8,128)(2,1)S(1)} %get-tuple-element.387), kind=kOutput, calls=%fused_computation.9.clone.1 | convolution fusion | flops 1115684864 | bytes 648192 | tf_op jit(solution)/shard_map/while/body/eval_jaxpr/bpk,ks->bps/dot_general | solution.py:57
  25.9 3.3 %fusion.88 = f32[1,512,256]{2,1,0:T(8,128)S(1)} fusion(s32[4096]{0:T(1024)} %get-tuple-element.392, f32[4096]{0:T(1024)} %get-tuple-element.389, f32[4096]{0:T(1024)} %get-tuple-element.386, bf16[8,1,8,4096]{3,2,1,0:T(8,128)(2,1)S(1)} %get-tuple-element.388, s32[]{:T(128)} %get-tuple-element.371, bf16[8,1,8,512]{3,2,1,0:T(8,128)(2,1)S(1)} %get-tuple-element.387), kind=kOutput, calls=%fused_computation.9.clone.1 | convolution fusion | flops 1115684864 | bytes 648192 | tf_op jit(solution)/shard_map/while/body/eval_jaxpr/bpk,ks->bps/dot_general | solution.py:57
  32.4 3.3 %fusion.88 = f32[1,512,256]{2,1,0:T(8,128)S(1)} fusion(s32[4096]{0:T(1024)} %get-tuple-element.392, f32[4096]{0:T(1024)} %get-tuple-element.389, f32[4096]{0:T(1024)} %get-tuple-element.386, bf16[8,1,8,4096]{3,2,1,0:T(8,128)(2,1)S(1)} %get-tuple-element.388, s32[]{:T(128)} %get-tuple-element.371, bf16[8,1,8,512]{3,2,1,0:T(8,128)(2,1)S(1)} %get-tuple-element.387), kind=kOutput, calls=%fused_computation.9.clone.1 | convolution fusion | flops 1115684864 | bytes 648192 | tf_op jit(solution)/shard_map/while/body/eval_jaxpr/bpk,ks->bps/dot_general | solution.py:57
  38.9 3.3 %fusion.88 = f32[1,512,256]{2,1,0:T(8,128)S(1)} fusion(s32[4096]{0:T(1024)} %get-tuple-element.392, f32[4096]{0:T(1024)} %get-tuple-element.389, f32[4096]{0:T(1024)} %get-tuple-element.386, bf16[8,1,8,4096]{3,2,1,0:T(8,128)(2,1)S(1)} %get-tuple-element.388, s32[]{:T(128)} %get-tuple-element.371, bf16[8,1,8,512]{3,2,1,0:T(8,128)(2,1)S(1)} %get-tuple-element.387), kind=kOutput, calls=%fused_computation.9.clone.1 | convolution fusion | flops 1115684864 | bytes 648192 | tf_op jit(solution)/shard_map/while/body/eval_jaxpr/bpk,ks->bps/dot_general | solution.py:57
  45.3 3.3 %fusion.88 = f32[1,512,256]{2,1,0:T(8,128)S(1)} fusion(s32[4096]{0:T(1024)} %get-tuple-element.392, f32[4096]{0:T(1024)} %get-tuple-element.389, f32[4096]{0:T(1024)} %get-tuple-element.386, bf16[8,1,8,4096]{3,2,1,0:T(8,128)(2,1)S(1)} %get-tuple-element.388, s32[]{:T(128)} %get-tuple-element.371, bf16[8,1,8,512]{3,2,1,0:T(8,128)(2,1)S(1)} %get-tuple-element.387), kind=kOutput, calls=%fused_computation.9.clone.1 | convolution fusion | flops 1115684864 | bytes 648192 | tf_op jit(solution)/shard_map/while/body/eval_jaxpr/bpk,ks->bps/dot_general | solution.py:57
  51.8 3.3 %fusion.88 = f32[1,512,256]{2,1,0:T(8,128)S(1)} fusion(s32[4096]{0:T(1024)} %get-tuple-element.392, f32[4096]{0:T(1024)} %get-tuple-element.389, f32[4096]{0:T(1024)} %get-tuple-element.386, bf16[8,1,8,4096]{3,2,1,0:T(8,128)(2,1)S(1)} %get-tuple-element.388, s32[]{:T(128)} %get-tuple-element.371, bf16[8,1,8,512]{3,2,1,0:T(8,128)(2,1)S(1)} %get-tuple-element.387), kind=kOutput, calls=%fused_computation.9.clone.1 | convolution fusion | flops 1115684864 | bytes 648192 | tf_op jit(solution)/shard_map/while/body/eval_jaxpr/bpk,ks->bps/dot_general | solution.py:57
  58.3 3.3 %fusion.88 = f32[1,512,256]{2,1,0:T(8,128)S(1)} fusion(s32[4096]{0:T(1024)} %get-tuple-element.392, f32[4096]{0:T(1024)} %get-tuple-element.389, f32[4096]{0:T(1024)} %get-tuple-element.386, bf16[8,1,8,4096]{3,2,1,0:T(8,128)(2,1)S(1)} %get-tuple-element.388, s32[]{:T(128)} %get-tuple-element.371, bf16[8,1,8,512]{3,2,1,0:T(8,128)(2,1)S(1)} %get-tuple-element.387), kind=kOutput, calls=%fused_computation.9.clone.1 | convolution fusion | flops 1115684864 | bytes 648192 | tf_op jit(solution)/shard_map/while/body/eval_jaxpr/bpk,ks->bps/dot_general | solution.py:57
  64.7 3.3 %fusion.88 = f32[1,512,256]{2,1,0:T(8,128)S(1)} fusion(s32[4096]{0:T(1024)} %get-tuple-element.392, f32[4096]{0:T(1024)} %get-tuple-element.389, f32[4096]{0:T(1024)} %get-tuple-element.386, bf16[8,1,8,4096]{3,2,1,0:T(8,128)(2,1)S(1)} %get-tuple-element.388, s32[]{:T(128)} %get-tuple-element.371, bf16[8,1,8,512]{3,2,1,0:T(8,128)(2,1)S(1)} %get-tuple-element.387), kind=kOutput, calls=%fused_computation.9.clone.1 | convolution fusion | flops 1115684864 | bytes 648192 | tf_op jit(solution)/shard_map/while/body/eval_jaxpr/bpk,ks->bps/dot_general | solution.py:57
  71.6 88.0 %all-gather.3.cloned.1.call-done = f32[64,1,512,128]{3,2,1,0:T(8,128)} async-done(((f32[8,1,512,128]{3,2,1,0:T(8,128)}), f32[64,1,512,128]{3,2,1,0:T(8,128)}) %all-gather.3.cloned.1.call-update) | async-done | bytes 16777232 | tf_op jit(solution)/shard_map/all_gather | solution.py:76
  159.7 8.3 %bitcast_reduce_fusion = f32[8,512,128]{2,1,0:T(8,128)} fusion(f32[8,8,512,128]{3,2,1,0:T(8,128)} %bitcast.119), kind=kLoop, calls=%fused_computation.64 | loop fusion | flops 3670016 | bytes 18874368 | tf_op jit(solution)/shard_map/reduce_sum | solution.py:76
  170.1 88.7 %while.27 = (s32[]{:T(128)}, f32[8,1,8,4096]{3,2,1,0:T(8,128)}, f32[8,1,8,512]{3,2,1,0:T(8,128)}, bf16[8,1,8,512]{3,2,1,0:T(8,128)(2,1)}, bf16[8,1,512,128]{3,2,...) while((s32[]{:T(128)}, f32[8,1,8,4096]{3,2,1,0:T(8,128)}, ...), condition=%wide.region_4.5_spmd.clone, body=%wide.region_3.4_spmd.clone.sunk | while | flops 1200193536 | bytes 30742168 | solution.py:101
  171.4 2.6 fusion.100
  182.5 2.6 fusion.100
  193.6 2.6 fusion.100
  200.8 2.6 fusion.102
  204.7 2.6 fusion.100
  211.8 2.6 fusion.102
  215.8 2.6 fusion.100
  222.9 2.6 fusion.102
  226.8 2.6 fusion.100
  237.9 2.6 fusion.100
  245.1 2.6 fusion.102
  249.0 2.6 fusion.100
  258.8 2.8 copy.18
  261.7 3.1 bitcast_bitcast_fusion
  264.7 2.7 reshape.171
  267.4 10.7 %all_to_all.33 = f32[4,1,8192]{2,1,0:T(1,128)S(1)} all-to-all(f32[4,1,8192]{2,1,0:T(1,128)S(1)} %reshape.171), channel_id=1, replica_groups=mesh['path'=4,'trade'=8] {'path'}, dimensions={0} | all-to-all | bytes 262144 | tf_op jit(solution)/shard_map/all_to_all | solution.py:107
  282.1 2.8 copy.19
  287.2 29.7 %reduce-scatter.2.cloned.1.call-done = f32[4,8,128]{2,1,0:T(8,128)} async-done(((f32[32,8,128]{2,1,0:T(8,128)}), f32[4,8,128]{2,1,0:T(8,128)}) %reduce-scatter.2.cloned.1.call-update) | async-done | bytes 16400 | tf_op jit(solution)/shard_map/reduce_scatter | solution.py:108
  (156 shorter events, 91.6 us)
Async XLA Ops:
  7.2 6.5 %copy-start = (bf16[32,8,4096]{2,1,0:T(8,128)(2,1)S(1)}, bf16[32,8,4096]{2,1,0:T(8,128)(2,1)}, u32[]{:S(2)}) copy-start(bf16[32,8,4096]{2,1,0:T(8,128)(2,1)} %param.14) | copy-start | bytes 6291460
  7.2 12.2 %all-to-all-start = ((bf16[32,8,128]{2,1,0:T(8,128)(2,1)}), bf16[32,8,128]{2,1,0:T(8,128)(2,1)S(1)}, u32[]{:S(2)}, u32[]{:S(2)}) async-start(bf16[32,8,128]{2,1,0:T(8,128)(2,1)} %param.13), calls=%async_computation | async-start | bytes 131072 | tf_op jit(solution)/shard_map/all_to_all | solution.py:29
  13.7 146.0 %all-gather.3.cloned.1.call-start = ((), (), s32[]{:S(2)}) async-start(), calls=%async_computation.4 | async-start | bytes 18874368 | tf_op jit(solution)/shard_map/all_gather | solution.py:76
  19.4 52.0 %copy-start.9 = (f32[32]{0:T(128)S(1)}, f32[32]{0:T(128)}, u32[]{:S(2)}) copy-start(f32[32]{0:T(128)} %param.17) | copy-start | bytes 388
  19.4 52.1 %copy-start.7 = (f32[128]{0:T(128)S(1)}, f32[128]{0:T(128)}, u32[]{:S(2)}) copy-start(f32[128]{0:T(128)} %param.18) | copy-start | bytes 1540
  19.5 4.0 %copy-start.8 = (f32[128]{0:T(128)S(1)}, f32[128]{0:T(128)}, u32[]{:S(2)}) copy-start(f32[128]{0:T(128)} %get-tuple-element.391) | copy-start | bytes 1540 | tf_op jit(solution)/shard_map/while
  19.5 5.3 %copy-start.4 = (s32[128]{0:T(128)S(1)}, s32[128]{0:T(128)}, u32[]{:S(2)}) copy-start(s32[128]{0:T(128)} %get-tuple-element.393) | copy-start | bytes 1540 | tf_op jit(solution)/shard_map/while
  25.9 4.0 %copy-start.8 = (f32[128]{0:T(128)S(1)}, f32[128]{0:T(128)}, u32[]{:S(2)}) copy-start(f32[128]{0:T(128)} %get-tuple-element.391) | copy-start | bytes 1540 | tf_op jit(solution)/shard_map/while
  25.9 5.3 %copy-start.4 = (s32[128]{0:T(128)S(1)}, s32[128]{0:T(128)}, u32[]{:S(2)}) copy-start(s32[128]{0:T(128)} %get-tuple-element.393) | copy-start | bytes 1540 | tf_op jit(solution)/shard_map/while
  32.4 4.0 %copy-start.8 = (f32[128]{0:T(128)S(1)}, f32[128]{0:T(128)}, u32[]{:S(2)}) copy-start(f32[128]{0:T(128)} %get-tuple-element.391) | copy-start | bytes 1540 | tf_op jit(solution)/shard_map/while
  32.4 5.3 %copy-start.4 = (s32[128]{0:T(128)S(1)}, s32[128]{0:T(128)}, u32[]{:S(2)}) copy-start(s32[128]{0:T(128)} %get-tuple-element.393) | copy-start | bytes 1540 | tf_op jit(solution)/shard_map/while
  38.8 4.0 %copy-start.8 = (f32[128]{0:T(128)S(1)}, f32[128]{0:T(128)}, u32[]{:S(2)}) copy-start(f32[128]{0:T(128)} %get-tuple-element.391) | copy-start | bytes 1540 | tf_op jit(solution)/shard_map/while
  38.9 5.3 %copy-start.4 = (s32[128]{0:T(128)S(1)}, s32[128]{0:T(128)}, u32[]{:S(2)}) copy-start(s32[128]{0:T(128)} %get-tuple-element.393) | copy-start | bytes 1540 | tf_op jit(solution)/shard_map/while
  45.3 5.3 %copy-start.4 = (s32[128]{0:T(128)S(1)}, s32[128]{0:T(128)}, u32[]{:S(2)}) copy-start(s32[128]{0:T(128)} %get-tuple-element.393) | copy-start | bytes 1540 | tf_op jit(solution)/shard_map/while
  51.8 4.0 %copy-start.8 = (f32[128]{0:T(128)S(1)}, f32[128]{0:T(128)}, u32[]{:S(2)}) copy-start(f32[128]{0:T(128)} %get-tuple-element.391) | copy-start | bytes 1540 | tf_op jit(solution)/shard_map/while
  51.8 5.3 %copy-start.4 = (s32[128]{0:T(128)S(1)}, s32[128]{0:T(128)}, u32[]{:S(2)}) copy-start(s32[128]{0:T(128)} %get-tuple-element.393) | copy-start | bytes 1540 | tf_op jit(solution)/shard_map/while
  58.3 5.3 %copy-start.4 = (s32[128]{0:T(128)S(1)}, s32[128]{0:T(128)}, u32[]{:S(2)}) copy-start(s32[128]{0:T(128)} %get-tuple-element.393) | copy-start | bytes 1540 | tf_op jit(solution)/shard_map/while
  64.7 4.0 %copy-start.8 = (f32[128]{0:T(128)S(1)}, f32[128]{0:T(128)}, u32[]{:S(2)}) copy-start(f32[128]{0:T(128)} %get-tuple-element.391) | copy-start | bytes 1540 | tf_op jit(solution)/shard_map/while
  64.7 5.3 %copy-start.4 = (s32[128]{0:T(128)S(1)}, s32[128]{0:T(128)}, u32[]{:S(2)}) copy-start(s32[128]{0:T(128)} %get-tuple-element.393) | copy-start | bytes 1540 | tf_op jit(solution)/shard_map/while
  71.2 88.5 %copy-start.1 = (bf16[8,1,8,4096]{3,2,1,0:T(8,128)(2,1)}, bf16[8,1,8,4096]{3,2,1,0:T(8,128)(2,1)S(1)}, u32[]{:S(2)}) copy-start(bf16[8,1,8,4096]{3,2,1,0:T(8,128)(2,1)S(1)} %get-tuple-element.431) | copy-start | bytes 1572868
  71.2 88.5 %copy-start.3 = (bf16[8,1,8,512]{3,2,1,0:T(8,128)(2,1)}, bf16[8,1,8,512]{3,2,1,0:T(8,128)(2,1)S(1)}, u32[]{:S(2)}) copy-start(bf16[8,1,8,512]{3,2,1,0:T(8,128)(2,1)S(1)} %get-tuple-element.438) | copy-start | bytes 196612
  71.2 245.7 %reduce-scatter.2.cloned.1.call-start = ((), (), s32[]{:S(2)}) async-start(), calls=%async_computation.3 | async-start | bytes 147456 | tf_op jit(solution)/shard_map/reduce_scatter | solution.py:108
  159.7 10.4 %copy-start.2 = (f32[4096]{0:T(1024)S(1)}, f32[4096]{0:T(1024)}, u32[]{:S(2)}) copy-start(f32[4096]{0:T(1024)} %get-tuple-element.436) | copy-start | bytes 49156
  159.7 10.4 %copy-start.5 = (s32[128]{0:T(128)S(1)}, s32[128]{0:T(128)}, u32[]{:S(2)}) copy-start(s32[128]{0:T(128)} %get-tuple-element.442) | copy-start | bytes 1540
  176.6 4.7 %copy-start.6 = (s32[128]{0:T(128)S(1)}, s32[128]{0:T(128)}, u32[]{:S(2)}) copy-start(s32[128]{0:T(128)} %get-tuple-element.454) | copy-start | bytes 1540 | tf_op jit(solution)/shard_map/while
  187.6 4.7 %copy-start.6 = (s32[128]{0:T(128)S(1)}, s32[128]{0:T(128)}, u32[]{:S(2)}) copy-start(s32[128]{0:T(128)} %get-tuple-element.454) | copy-start | bytes 1540 | tf_op jit(solution)/shard_map/while
  198.7 4.7 %copy-start.6 = (s32[128]{0:T(128)S(1)}, s32[128]{0:T(128)}, u32[]{:S(2)}) copy-start(s32[128]{0:T(128)} %get-tuple-element.454) | copy-start | bytes 1540 | tf_op jit(solution)/shard_map/while
  209.8 4.7 %copy-start.6 = (s32[128]{0:T(128)S(1)}, s32[128]{0:T(128)}, u32[]{:S(2)}) copy-start(s32[128]{0:T(128)} %get-tuple-element.454) | copy-start | bytes 1540 | tf_op jit(solution)/shard_map/while
  220.9 4.7 %copy-start.6 = (s32[128]{0:T(128)S(1)}, s32[128]{0:T(128)}, u32[]{:S(2)}) copy-start(s32[128]{0:T(128)} %get-tuple-element.454) | copy-start | bytes 1540 | tf_op jit(solution)/shard_map/while
  232.0 4.7 %copy-start.6 = (s32[128]{0:T(128)S(1)}, s32[128]{0:T(128)}, u32[]{:S(2)}) copy-start(s32[128]{0:T(128)} %get-tuple-element.454) | copy-start | bytes 1540 | tf_op jit(solution)/shard_map/while
  243.1 4.7 %copy-start.6 = (s32[128]{0:T(128)S(1)}, s32[128]{0:T(128)}, u32[]{:S(2)}) copy-start(s32[128]{0:T(128)} %get-tuple-element.454) | copy-start | bytes 1540 | tf_op jit(solution)/shard_map/while
  254.1 4.7 %copy-start.6 = (s32[128]{0:T(128)S(1)}, s32[128]{0:T(128)}, u32[]{:S(2)}) copy-start(s32[128]{0:T(128)} %get-tuple-element.454) | copy-start | bytes 1540 | tf_op jit(solution)/shard_map/while
  (2 other events, 7.9 us)
Sparse Core Ops, SparseCore 0:
  71.3 88.2 all-gather.2
  285.1 31.8 reduce-scatter.1
